TPU v7x, 32 devices: a whole 2x2x4 slice. The times are simulated.
32 devices in a mesh: section: 4 (over y, core), batch: 8 (over z, x).
Axes of the slice: x: 2, y: 2, z: 4, core: 2. Of those that a mesh axis runs over, the one named last changes fastest.
Arguments:
- masters: float32 [32, 512, 1024], P('section', 'batch'), may hold values from -0.1875 to 0.1875
- first_moment: float32 [32, 512, 1024], P('section', 'batch')
- second_moment: float32 [32, 512, 1024], P('section', 'batch')
- section_table: float32 [8, 6144], P('section'), may hold values from -1.2 to 1.2
- table_first: float32 [8, 6144], P('section')
- table_second: float32 [8, 6144], P('section')
- owners: int32 [29], replicated, may hold values from 0 to 31, as said below
- step_count: int32 [1], replicated, may hold values from 2 to 20
- phones: int32 [64, 512], P(('section', 'batch')), may hold values from 0 to 511
- codes: int32 [64, 512, 8], P(('section', 'batch')), may hold values from 0 to 1023
- segments: int32 [64, 512], P(('section', 'batch')), may hold values from 0 to 2, never falling along the last dimension, each value on 1 to 384 neighbouring positions
- sections: int32 [64, 1], P(('section', 'batch')), may hold values from 0 to 7
- targets: int32 [64, 512], P(('section', 'batch')), may hold values from 0 to 1023
Outputs:
- new_masters: float32 [32, 512, 1024], P('section', 'batch')
- new_first: float32 [32, 512, 1024], P('section', 'batch')
- new_second: float32 [32, 512, 1024], P('section', 'batch')
- new_table: float32 [8, 6144], P('section')
- new_table_first: float32 [8, 6144], P('section')
- new_table_second: float32 [8, 6144], P('section')
- grad_norm: float32 [], replicated
- loss: float32 [], replicated
Inputs may be any that keep to these rules, and one draw needn't show every extreme that they name: `owners`: distinct slot numbers; slot 0 and slot 31 are always among them; a section index of the slots owns a varying number of blocks. `sections`: every section is the section of some row; rows of one section may stand on any device.
All inputs are finite; a program needn't handle non-finite values.
Results may differ from a plain program's by a relative error of at most 0.0067.
Values may be sent and summed in bfloat16 or wider, within the bound.
A program may use at most 320 MiB of HBM per device.

v0:
```python
import math
import jax
import jax.numpy as jnp
from jax import lax
from jax.sharding import PartitionSpec as P

D = 1024
HEADS = 16
HD = 64
FF = 4096
CODES = 1024
LEVELS = 8
PHONES = 512
SECTIONS = 8
clip_limit = 0.002
learn_rate = 0.02
table_rate = 0.1
beta_one = 0.9
beta_two = 0.95
adam_eps = 1e-08
decay_rate = 0.1
norm_eps = 1e-05
pos_scale = 0.1
exact = lax.Precision.HIGHEST
float_out = jnp.float32


def positions(segs):
    index = jnp.broadcast_to(jnp.arange(segs.shape[-1], dtype=jnp.int32), segs.shape)
    first = jnp.ones(segs.shape[:-1] + (1,), dtype=bool)
    change = jnp.concatenate([first, segs[..., 1:] != segs[..., :-1]], axis=-1)
    starts = lax.cummax(jnp.where(change, index, jnp.zeros_like(index)), axis=segs.ndim - 1)
    return (index - starts).astype(jnp.float32)


def sinusoid(place, width):
    column = jnp.arange(width)
    rate = jnp.exp(-(2 * (column // 2)).astype(jnp.float32) * (math.log(10000.0) / width))
    angle = place[..., None] * rate
    return pos_scale * jnp.where(column % 2 == 0, jnp.sin(angle), jnp.cos(angle))


def normalize(stream):
    centred = stream - jnp.mean(stream, axis=-1, keepdims=True)
    scale = lax.rsqrt(jnp.mean(centred * centred, axis=-1, keepdims=True) + norm_eps)
    return (centred * scale, scale)


def norm_back(grad, normed, scale, gain):
    inner = grad * (1.0 + gain)
    result = scale * (
        inner
        - jnp.mean(inner, axis=-1, keepdims=True)
        - normed * jnp.mean(inner * normed, axis=-1, keepdims=True)
    )
    return (result, jnp.sum(grad * normed, axis=1), jnp.sum(grad, axis=1))


def unpack(blocks):
    half = blocks.shape[1]
    width = blocks.shape[2]
    code_w = blocks[0:2].reshape(2 * half, width)
    phone_w = blocks[2]
    head_w = blocks[3:5].reshape(width, 2 * half)
    qkv_w = blocks[5:11].reshape(3, width, width)
    out_w = blocks[11:13].reshape(width, width)
    up_w = blocks[13:21].reshape(4, width, width)
    down_w = blocks[21:29].reshape(4 * width, width)
    return (code_w, phone_w, head_w, qkv_w, out_w, up_w, down_w)


def pack(pieces, half, width):
    return jnp.concatenate([piece.reshape(-1, half, width) for piece in pieces], axis=0)


def attend_scores(queries, key_vecs, same):
    scores = jnp.einsum(
        "rlhe,rmhe->rhlm", queries, key_vecs, preferred_element_type=float_out
    ) * HD ** (-0.5)
    return jnp.where(same[:, None], scores, -1000000000.0)


def forward(matrices, params, phones, codes, segments, section_ids, targets, section_hot):
    code_w, phone_w, head_w, qkv_w, out_w, up_w, down_w = matrices
    rows, length = segments.shape
    levels = (jnp.arange(LEVELS)[None, :] <= section_ids[:, None]).astype(jnp.bfloat16)
    vocab = jnp.arange(CODES)
    multi = jnp.zeros((rows, length, CODES), jnp.bfloat16)
    for level in range(LEVELS):
        multi = (
            multi
            + (codes[:, :, level, None] == vocab).astype(jnp.bfloat16)
            * levels[:, level, None, None]
        )
    phone_hot = (phones[:, :, None] == jnp.arange(PHONES)).astype(jnp.bfloat16)
    stream = jnp.einsum("rlc,cd->rld", multi, code_w, preferred_element_type=float_out)
    stream = stream + jnp.einsum(
        "rlp,pd->rld", phone_hot, phone_w, preferred_element_type=float_out
    )
    stream = stream + sinusoid(positions(segments), D)
    normed_one, scale_one = normalize(stream)
    input_one = (normed_one * (1.0 + params[:, 0]) + params[:, 1]).astype(jnp.bfloat16)
    qkv = jnp.einsum("rld,kde->krle", input_one, qkv_w, preferred_element_type=float_out).astype(
        jnp.bfloat16
    )
    heads = qkv.reshape(3, rows, length, HEADS, HD)
    same = segments[:, :, None] == segments[:, None, :]
    scores = attend_scores(heads[0], heads[1], same)
    log_total = jax.nn.logsumexp(scores, axis=-1)
    probs = jnp.exp(scores - log_total[..., None]).astype(jnp.bfloat16)
    mixed = jnp.einsum("rhlm,rmhe->rlhe", probs, heads[2], preferred_element_type=float_out)
    mixed = mixed.astype(jnp.bfloat16).reshape(rows, length, D)
    stream = stream + jnp.einsum("rld,de->rle", mixed, out_w, preferred_element_type=float_out)
    normed_two, scale_two = normalize(stream)
    input_two = (normed_two * (1.0 + params[:, 2]) + params[:, 3]).astype(jnp.bfloat16)
    hidden = jnp.einsum("rld,gde->rlge", input_two, up_w, preferred_element_type=float_out)
    active = jax.nn.gelu(hidden, approximate=False).astype(jnp.bfloat16).reshape(rows, length, FF)
    stream = stream + jnp.einsum("rlf,fd->rld", active, down_w, preferred_element_type=float_out)
    normed_three, scale_three = normalize(stream)
    input_three = (normed_three * (1.0 + params[:, 4]) + params[:, 5]).astype(jnp.bfloat16)
    logits = jnp.einsum("rld,dc->rlc", input_three, head_w, preferred_element_type=float_out)
    log_norm = jax.nn.logsumexp(logits, axis=-1)
    target_hot = (targets[:, :, None] == vocab).astype(jnp.float32)
    losses = log_norm - jnp.sum(logits * target_hot, axis=-1)
    section_loss = jnp.sum(section_hot * jnp.sum(losses, axis=1)[:, None], axis=0)
    kept = (
        multi,
        phone_hot,
        normed_one,
        scale_one,
        input_one,
        heads,
        same,
        log_total,
        mixed,
        normed_two,
        scale_two,
        input_two,
        hidden,
        active,
        normed_three,
        scale_three,
        input_three,
        logits,
        log_norm,
        target_hot,
    )
    return (kept, section_loss)


def backward(matrices, params, kept, row_weight):
    code_w, phone_w, head_w, qkv_w, out_w, up_w, down_w = matrices
    (
        multi,
        phone_hot,
        normed_one,
        scale_one,
        input_one,
        heads,
        same,
        log_total,
        mixed,
        normed_two,
        scale_two,
        input_two,
        hidden,
        active,
        normed_three,
        scale_three,
        input_three,
        logits,
        log_norm,
        target_hot,
    ) = kept
    rows, length = (same.shape[0], same.shape[1])
    predicted = jnp.exp(logits - log_norm[..., None])
    grad_logits = ((predicted - target_hot) * row_weight[:, None, None]).astype(jnp.bfloat16)
    grad_head = jnp.einsum(
        "rld,rlc->dc", input_three, grad_logits, preferred_element_type=float_out
    )
    grad_three = jnp.einsum("rlc,dc->rld", grad_logits, head_w, preferred_element_type=float_out)
    grad_stream, gain_three, shift_three = norm_back(
        grad_three, normed_three, scale_three, params[:, 4]
    )
    grad_ffn = grad_stream.astype(jnp.bfloat16)
    grad_down = jnp.einsum("rlf,rld->fd", active, grad_ffn, preferred_element_type=float_out)
    grad_active = jnp.einsum("rld,fd->rlf", grad_ffn, down_w, preferred_element_type=float_out)
    _, gelu_pull = jax.vjp(lambda value: jax.nn.gelu(value, approximate=False), hidden)
    grad_hidden = gelu_pull(grad_active.reshape(hidden.shape))[0].astype(jnp.bfloat16)
    grad_up = jnp.einsum("rld,rlge->gde", input_two, grad_hidden, preferred_element_type=float_out)
    grad_two = jnp.einsum("rlge,gde->rld", grad_hidden, up_w, preferred_element_type=float_out)
    grad_norm_two, gain_two, shift_two = norm_back(grad_two, normed_two, scale_two, params[:, 2])
    grad_stream = grad_stream + grad_norm_two
    grad_attn = grad_stream.astype(jnp.bfloat16)
    grad_out = jnp.einsum("rld,rle->de", mixed, grad_attn, preferred_element_type=float_out)
    grad_mixed = jnp.einsum("rle,de->rld", grad_attn, out_w, preferred_element_type=float_out)
    grad_mixed = grad_mixed.astype(jnp.bfloat16).reshape(rows, length, HEADS, HD)
    scores = attend_scores(heads[0], heads[1], same)
    probs = jnp.exp(scores - log_total[..., None])
    probs_low = probs.astype(jnp.bfloat16)
    grad_values = jnp.einsum(
        "rhlm,rlhe->rmhe", probs_low, grad_mixed, preferred_element_type=float_out
    )
    grad_probs = jnp.einsum(
        "rlhe,rmhe->rhlm", grad_mixed, heads[2], preferred_element_type=float_out
    )
    grad_scores = (
        probs * (grad_probs - jnp.sum(probs * grad_probs, axis=-1, keepdims=True))
    ).astype(jnp.bfloat16)
    grad_queries = jnp.einsum(
        "rhlm,rmhe->rlhe", grad_scores, heads[1], preferred_element_type=float_out
    ) * HD ** (-0.5)
    grad_key_vecs = jnp.einsum(
        "rhlm,rlhe->rmhe", grad_scores, heads[0], preferred_element_type=float_out
    ) * HD ** (-0.5)
    grad_qkv = (
        jnp.stack([grad_queries, grad_key_vecs, grad_values])
        .reshape(3, rows, length, D)
        .astype(jnp.bfloat16)
    )
    grad_proj = jnp.einsum("rld,krle->kde", input_one, grad_qkv, preferred_element_type=float_out)
    grad_one = jnp.einsum("krle,kde->rld", grad_qkv, qkv_w, preferred_element_type=float_out)
    grad_norm_one, gain_one, shift_one = norm_back(grad_one, normed_one, scale_one, params[:, 0])
    grad_embed = (grad_stream + grad_norm_one).astype(jnp.bfloat16)
    grad_code = jnp.einsum("rlc,rld->cd", multi, grad_embed, preferred_element_type=float_out)
    grad_phone = jnp.einsum("rlp,rld->pd", phone_hot, grad_embed, preferred_element_type=float_out)
    half = phone_w.shape[0]
    block_grads = pack(
        (grad_code, grad_phone, grad_head, grad_proj, grad_out, grad_up, grad_down), half, D
    )
    row_grads = jnp.stack(
        [gain_one, shift_one, gain_two, shift_two, gain_three, shift_three], axis=1
    )
    return (block_grads, row_grads)


def adam(weight, first, second, grad, rate, step):
    new_first = beta_one * first + (1.0 - beta_one) * grad
    new_second = beta_two * second + (1.0 - beta_two) * grad * grad
    fix_one = 1.0 - jnp.power(beta_one, step)
    fix_two = 1.0 - jnp.power(beta_two, step)
    update = new_first / fix_one / (jnp.sqrt(new_second / fix_two) + adam_eps)
    return (weight - rate * (update + decay_rate * weight), new_first, new_second)


def per_device(
    masters,
    first_moment,
    second_moment,
    section_table,
    table_first,
    table_second,
    owners,
    step_count,
    phones,
    codes,
    segments,
    sections,
    targets,
):
    section_width = lax.axis_size("section")
    batch_width = lax.axis_size("batch")
    section_ids = sections[:, 0]
    row_count = section_ids.shape[0]
    section_hot = (section_ids[:, None] == jnp.arange(SECTIONS)[None, :]).astype(jnp.float32)
    local_counts = jnp.sum(section_hot, axis=0) * segments.shape[1]
    shard_rows = lax.all_gather(masters.astype(jnp.bfloat16), "batch", axis=1, tiled=True)
    all_slots = lax.all_gather(shard_rows, "section", axis=0, tiled=True)
    blocks = jnp.take(all_slots, owners, axis=0)
    table = lax.all_gather(section_table, "section", axis=0, tiled=True)
    matrices = unpack(blocks)
    params = jnp.einsum("rs,sk->rk", section_hot, table, precision=exact).reshape(
        row_count, 6, 1, D
    )
    kept, section_loss = forward(
        matrices, params, phones, codes, segments, section_ids, targets, section_hot
    )
    counts, loss_sums = lax.psum((local_counts, section_loss), ("section", "batch"))
    row_weight = jnp.sum(section_hot / (SECTIONS * counts)[None, :], axis=1)
    block_grads, row_grads = backward(matrices, params, kept, row_weight)
    table_local = jnp.einsum(
        "rs,rk->sk", section_hot, row_grads.reshape(row_count, 6 * D), precision=exact
    )
    table_sum = lax.psum(table_local, ("section", "batch"))
    own_count = section_table.shape[0]
    table_grad = lax.dynamic_slice_in_dim(
        table_sum, lax.axis_index("section") * own_count, own_count, 0
    )
    per_group = masters.shape[0]
    piece_rows = masters.shape[1]
    split_grads = block_grads.reshape(block_grads.shape[0], batch_width, piece_rows, D)
    group_of = owners // per_group
    within = owners % per_group
    target_slot = (
        (group_of * batch_width)[:, None] * per_group
        + jnp.arange(batch_width)[None, :] * per_group
        + within[:, None]
    )
    arranged = jnp.zeros((section_width * batch_width * per_group, piece_rows, D), jnp.float32)
    arranged = arranged.at[target_slot.reshape(-1)].set(split_grads.reshape(-1, piece_rows, D))
    own_grad = lax.psum_scatter(arranged, ("section", "batch"), scatter_dimension=0, tiled=True)
    square_sum = jnp.sum(own_grad * own_grad) + jnp.sum(table_grad * table_grad) / batch_width
    grad_norm = jnp.sqrt(lax.psum(square_sum, ("section", "batch")))
    clip_factor = jnp.minimum(1.0, clip_limit / grad_norm)
    step = step_count[0].astype(jnp.float32)
    new_masters, new_first, new_second = adam(
        masters, first_moment, second_moment, own_grad * clip_factor, learn_rate, step
    )
    new_table, new_table_first, new_table_second = adam(
        section_table, table_first, table_second, table_grad * clip_factor, table_rate, step
    )
    loss = jnp.sum(loss_sums / (SECTIONS * counts))
    return (
        new_masters,
        new_first,
        new_second,
        new_table,
        new_table_first,
        new_table_second,
        grad_norm,
        loss,
    )


def solution(mesh):
    return jax.shard_map(
        per_device,
        mesh=mesh,
        in_specs=(
            P("section", "batch", None),
            P("section", "batch", None),
            P("section", "batch", None),
            P("section", None),
            P("section", None),
            P("section", None),
            P(),
            P(),
            P(("section", "batch"), None),
            P(("section", "batch"), None, None),
            P(("section", "batch"), None),
            P(("section", "batch"), None),
            P(("section", "batch"), None),
        ),
        out_specs=(
            P("section", "batch", None),
            P("section", "batch", None),
            P("section", "batch", None),
            P("section", None),
            P("section", None),
            P("section", None),
            P(),
            P(),
        ),
        check_vma=False,
    )
```

profile of v0, /device:TPU:0, one launch (start us, length us, event | category | flops | bytes accessed | tf_op | source)
XLA Modules:
  0.0 2446.3 jit_solution(5869725408270620591)
XLA Ops:
  10.0 128.4 %all-gather.4.cloned.1.call-done = bf16[8,512,1024]{2,1,0:T(8,128)(2,1)} async-done(((bf16[8,64,1024]{2,1,0:T(8,128)(2,1)}), bf16[8,512,1024]{2,1,0:T(8,128)(2,1)}) %all-gather.4.cloned.1.call-update) | async-done | bytes 8388624 | tf_op jit(solution)/shard_map/all_gather | solution.py:267
  139.2 38.7 %psum.28 = f32[8]{0:T(128)S(1)} all-reduce(f32[8]{0:T(128)S(1)} %broadcast_multiply_fusion.10), channel_id=1, replica_groups=mesh['section'=4,'batch'=8] {'section','batch'}, use_global_device_ids=true, to_apply=%region_13.14 | all-reduce | flops 8 | bytes 64 | tf_op jit(solution)/shard_map/psum | solution.py:278
  179.1 7.4 all-gather
  189.8 151.7 %all-gather.6.cloned.1.call-done = bf16[32,512,1024]{2,1,0:T(8,128)(2,1)} async-done(((bf16[8,512,1024]{2,1,0:T(8,128)(2,1)}), bf16[32,512,1024]{2,1,0:T(8,128)(2,1)}) %all-gather.6.cloned.1.call-update) | async-done | bytes 33554448 | tf_op jit(solution)/shard_map/all_gather | solution.py:268
  341.5 22.0 gather_fusion
  363.5 20.5 broadcast_select_fusion
  384.0 5.7 fusion.89
  389.7 3.5 slice.160
  393.2 14.0 fusion.88
  407.4 6.3 fusion.82
  413.7 17.8 fusion.92
  433.5 10.1 convert_bitcast_fusion
  443.6 3.3 fusion.90
  446.9 13.8 fusion
  460.7 14.1 exponential_reduce_fusion
  474.9 15.6 convolution_convert_fusion.2
  490.5 6.3 fusion.93
  497.4 49.3 %multiply_convert_fusion.1 = (bf16[2,512,4,1024]{3,1,2,0:T(8,128)(2,1)}, f32[2,512,4,1024]{3,1,2,0:T(8,128)}, f32[2,512,4,1024]{3,1,2,0:T(8,128)}) fusion(bf16[4,1024,1024,1]{2,1,0,3:T(8,128)(2,1)S(1)} %bitcast.258, f32[2,512,1024]{2,1,0:T(8,128)S(1)} %get-tuple-element.74, f32[2,1024]{1,0:T(2,128)S(1)} %get-tuple-element.95, ...), kind=kOutput, calls=%fused_computation.14 | convolution fusion | flops 8867807232 | bytes 54550528 | tf_op jit(solution)/shard_map/rld,gde->rlge/dot_general | solution.py:116
  546.7 11.4 copy.71
  558.1 14.7 fusion.94
  580.9 4.0 multiply_reduce_fusion.1
  586.1 24.3 add_convert_fusion
  610.4 16.0 fusion.12
  629.8 3.7 convolution_convert_fusion.1
  633.5 2.9 copy.73
  636.5 25.7 %multiply_reduce_fusion = (f32[2,16,512]{2,1,0:T(8,128)S(1)}, f32[2,16,512,512]{2,3,1,0:T(8,128)}) fusion(f32[2,16,512,512]{2,3,1,0:T(8,128)} %get-tuple-element.72, f32[2,16,512]{2,1,0:T(8,128)S(1)} %copy-done.30, pred[2,512,512]{1,2,0:T(8,128)(4,1)S(1)} %copy-done.3, bf16[2,512,16,64]{1,3,2,0:T(8,128)(2,1)S(1)} %bitcast.243, ...), kind=kOutput, calls=%fused_computation.3 | convolution fusion | flops 1115668480 | bytes 71958528 | tf_op jit(solution)/shard_map/rlhe,rmhe->rhlm/dot_general | solution.py:204
  662.2 28.4 %multiply_convert_fusion = bf16[2,16,512,512]{2,3,1,0:T(8,128)(2,1)} fusion(f32[2,16,512,512]{2,3,1,0:T(8,128)} %get-tuple-element.83, f32[2,16,512,512]{2,3,1,0:T(8,128)} %get-tuple-element.72, f32[2,16,512]{2,1,0:T(8,128)S(1)} %get-tuple-element.82, f32[2,16,512]{2,1,0:T(8,128)S(1)} %copy-done.30, pred[2,512,512]{1,2,0:T(8,128)(4,1)S(1)} %copy-done.3), kind=kLoop, calls=%fused_computation.2 | loop fusion | flops 50331648 | bytes 84541440 | tf_op jit(solution)/shard_map/convert_element_type | solution.py:209
  690.6 9.9 multiply_convert_fusion.3
  700.5 13.0 multiply_convert_fusion.2
  713.5 16.2 convolution_convert_fusion
  729.7 23.3 fusion.76
  753.1 5.4 fusion.49
  760.9 4.1 copy.78
  765.0 3.9 copy.79
  769.0 14.8 fusion.23
  783.9 9.2 fusion.11
  794.3 5.5 add_convert_fusion.1
  800.1 5.5 fusion.80
  812.8 12.1 constant_dynamic-update-slice_fusion.1
  824.9 4.3 bitcast_dynamic-update-slice_fusion.1
  829.2 13.1 constant_dynamic-update-slice_fusion
  842.3 12.3 bitcast_dynamic-update-slice_fusion
  854.6 21.3 broadcast_in_dim.44
  875.9 107.0 %scatter_fusion = f32[256,64,1024]{2,1,0:T(8,128)} fusion(f32[256,64,1024]{2,1,0:T(8,128)} %broadcast_in_dim.44, s32[232]{0:T(256)S(1)} %bitcast.280, f32[232,64,1024]{2,1,0:T(8,128)} %bitcast.238), kind=kCustom, calls=%fused_computation.1 | custom fusion | bytes 182453152 | tf_op jit(solution)/shard_map/scatter | solution.py:300
  986.1 1399.5 %reduce-scatter.2.cloned.1.call-done = f32[8,64,1024]{2,1,0:T(8,128)} async-done(((f32[256,64,1024]{2,1,0:T(8,128)}), f32[8,64,1024]{2,1,0:T(8,128)}) %reduce-scatter.2.cloned.1.call-update) | async-done | bytes 2097168 | tf_op jit(solution)/shard_map/reduce_scatter | solution.py:301
  2385.6 2.7 multiply_reduce_fusion.9
  2389.0 39.4 %all-reduce.1 = (f32[]{:T(128)}, f32[8]{0:T(128)S(1)}) all-reduce(f32[]{:T(128)S(6)} %add.310, f32[8]{0:T(128)S(1)} %copy-done.99), channel_id=1, replica_groups=mesh['section'=4,'batch'=8] {'section','batch'}, use_global_device_ids=true, to_apply=%region_33.34 | all-reduce | flops 9 | bytes 72 | tf_op jit(solution)/shard_map/psum | solution.py:303
  2431.5 6.9 multiply_subtract_fusion
  (316 shorter events, 37.9 us)
Async XLA Ops:
  7.2 131.2 %all-gather.4.cloned.1.call-start = ((), (), s32[]{:S(2)}) async-start(), calls=%async_computation.1 | async-start | bytes 9437184 | tf_op jit(solution)/shard_map/all_gather | solution.py:267
  10.0 331.5 %all-gather.6.cloned.1.call-start = ((), (), s32[]{:S(2)}) async-start(), calls=%async_computation.2 | async-start | bytes 41943040 | tf_op jit(solution)/shard_map/all_gather | solution.py:268
  138.4 39.5 %copy-start.33 = (s32[2,512]{1,0:T(2,128)S(1)}, s32[2,512]{1,0:T(2,128)}, u32[]{:S(2)}) copy-start(s32[2,512]{1,0:T(2,128)} %param.23) | copy-start | bytes 12292
  138.4 40.7 %copy-start.31 = (f32[2,6144]{1,0:T(2,128)S(1)}, f32[2,6144]{1,0:T(2,128)}, u32[]{:S(2)}) copy-start(f32[2,6144]{1,0:T(2,128)} %param.16) | copy-start | bytes 147460
  138.4 48.6 %copy-start.103 = (s32[29]{0:T(128)S(1)}, s32[29]{0:T(128)}, u32[]{:S(2)}) copy-start(s32[29]{0:T(128)} %param.19) | copy-start | bytes 352
  138.4 50.1 %copy-start.42 = (s32[2,512,8]{1,2,0:T(8,128)S(1)}, s32[2,512,8]{1,2,0:T(8,128)}, u32[]{:S(2)}) copy-start(s32[2,512,8]{1,2,0:T(8,128)} %param.22) | copy-start | bytes 98308
  138.4 845.4 %all-reduce.4.cloned.1.call-start = ((), (), s32[]{:S(2)}) async-start(), calls=%async_computation.4 | async-start | bytes 393216 | tf_op jit(solution)/shard_map/psum | solution.py:284
  188.4 218.9 %copy-start.83 = (bf16[2]{0:T(256)(128)(2,1)}, bf16[2]{0:T(256)(128)(2,1)S(1)}, u32[]{:S(2)}) copy-start(bf16[2]{0:T(256)(128)(2,1)S(1)} %get-tuple-element.58) | copy-start | bytes 16
  188.4 218.9 %copy-start.85 = (bf16[2]{0:T(256)(128)(2,1)}, bf16[2]{0:T(256)(128)(2,1)S(1)}, u32[]{:S(2)}) copy-start(bf16[2]{0:T(256)(128)(2,1)S(1)} %get-tuple-element.59) | copy-start | bytes 16
  188.4 218.9 %copy-start.87 = (bf16[2]{0:T(256)(128)(2,1)}, bf16[2]{0:T(256)(128)(2,1)S(1)}, u32[]{:S(2)}) copy-start(bf16[2]{0:T(256)(128)(2,1)S(1)} %get-tuple-element.60) | copy-start | bytes 16
  188.4 218.9 %copy-start.89 = (bf16[2]{0:T(256)(128)(2,1)}, bf16[2]{0:T(256)(128)(2,1)S(1)}, u32[]{:S(2)}) copy-start(bf16[2]{0:T(256)(128)(2,1)S(1)} %get-tuple-element.61) | copy-start | bytes 16
  188.4 218.9 %copy-start.91 = (bf16[2]{0:T(256)(128)(2,1)}, bf16[2]{0:T(256)(128)(2,1)S(1)}, u32[]{:S(2)}) copy-start(bf16[2]{0:T(256)(128)(2,1)S(1)} %get-tuple-element.62) | copy-start | bytes 16
  188.4 218.9 %copy-start.93 = (bf16[2]{0:T(256)(128)(2,1)}, bf16[2]{0:T(256)(128)(2,1)S(1)}, u32[]{:S(2)}) copy-start(bf16[2]{0:T(256)(128)(2,1)S(1)} %get-tuple-element.63) | copy-start | bytes 16
  188.4 218.9 %copy-start.95 = (bf16[2]{0:T(256)(128)(2,1)}, bf16[2]{0:T(256)(128)(2,1)S(1)}, u32[]{:S(2)}) copy-start(bf16[2]{0:T(256)(128)(2,1)S(1)} %get-tuple-element.64) | copy-start | bytes 16
  188.4 218.9 %copy-start.97 = (bf16[2]{0:T(256)(128)(2,1)}, bf16[2]{0:T(256)(128)(2,1)S(1)}, u32[]{:S(2)}) copy-start(bf16[2]{0:T(256)(128)(2,1)S(1)} %get-tuple-element.65) | copy-start | bytes 16
  188.6 218.8 %copy-start.63 = (s32[2,512]{1,0:T(2,128)}, s32[2,512]{1,0:T(2,128)S(1)}, u32[]{:S(2)}) copy-start(s32[2,512]{1,0:T(2,128)S(1)} %get-tuple-element.85) | copy-start | bytes 12292
  188.6 218.8 %copy-start.65 = (s32[2,512]{1,0:T(2,128)}, s32[2,512]{1,0:T(2,128)S(1)}, u32[]{:S(2)}) copy-start(s32[2,512]{1,0:T(2,128)S(1)} %get-tuple-element.86) | copy-start | bytes 12292
  188.6 218.8 %copy-start.67 = (s32[2,512]{1,0:T(2,128)}, s32[2,512]{1,0:T(2,128)S(1)}, u32[]{:S(2)}) copy-start(s32[2,512]{1,0:T(2,128)S(1)} %get-tuple-element.87) | copy-start | bytes 12292
  188.6 218.8 %copy-start.69 = (s32[2,512]{1,0:T(2,128)}, s32[2,512]{1,0:T(2,128)S(1)}, u32[]{:S(2)}) copy-start(s32[2,512]{1,0:T(2,128)S(1)} %get-tuple-element.88) | copy-start | bytes 12292
  188.7 218.7 %copy-start.71 = (s32[2,512]{1,0:T(2,128)}, s32[2,512]{1,0:T(2,128)S(1)}, u32[]{:S(2)}) copy-start(s32[2,512]{1,0:T(2,128)S(1)} %get-tuple-element.89) | copy-start | bytes 12292
  188.7 218.7 %copy-start.73 = (s32[2,512]{1,0:T(2,128)}, s32[2,512]{1,0:T(2,128)S(1)}, u32[]{:S(2)}) copy-start(s32[2,512]{1,0:T(2,128)S(1)} %get-tuple-element.90) | copy-start | bytes 12292
  188.7 218.7 %copy-start.75 = (s32[2,512]{1,0:T(2,128)}, s32[2,512]{1,0:T(2,128)S(1)}, u32[]{:S(2)}) copy-start(s32[2,512]{1,0:T(2,128)S(1)} %get-tuple-element.91) | copy-start | bytes 12292
  188.7 218.7 %copy-start.77 = (s32[2,512]{1,0:T(2,128)}, s32[2,512]{1,0:T(2,128)S(1)}, u32[]{:S(2)}) copy-start(s32[2,512]{1,0:T(2,128)S(1)} %get-tuple-element.92) | copy-start | bytes 12292
  188.8 243.3 %copy-start.40 = (f32[2,1024]{1,0:T(2,128)}, f32[2,1024]{1,0:T(2,128)S(1)}, u32[]{:S(2)}) copy-start(f32[2,1024]{1,0:T(2,128)S(1)} %get-tuple-element.98) | copy-start | bytes 24580
  188.8 243.3 %copy-start.56 = (f32[2,1024]{1,0:T(2,128)}, f32[2,1024]{1,0:T(2,128)S(1)}, u32[]{:S(2)}) copy-start(f32[2,1024]{1,0:T(2,128)S(1)} %get-tuple-element.97) | copy-start | bytes 24580
  188.8 308.5 %copy-start.60 = (f32[2,1024]{1,0:T(2,128)}, f32[2,1024]{1,0:T(2,128)S(1)}, u32[]{:S(2)}) copy-start(f32[2,1024]{1,0:T(2,128)S(1)} %get-tuple-element.95) | copy-start | bytes 24580
  189.8 285.0 %copy-start.2 = (pred[2,512,512]{1,2,0:T(8,128)(4,1)}, pred[2,512,512]{1,2,0:T(8,128)(4,1)S(1)}, u32[]{:S(2)}) copy-start(pred[2,512,512]{1,2,0:T(8,128)(4,1)S(1)} %broadcast_compare_fusion) | copy-start | bytes 1572868
  393.2 38.9 %copy-start.20 = (bf16[6,512,1024]{2,1,0:T(8,128)(2,1)}, bf16[6,512,1024]{2,1,0:T(8,128)(2,1)S(1)}, u32[]{:S(2)}) copy-start(bf16[6,512,1024]{2,1,0:T(8,128)(2,1)S(1)} %slice.160) | copy-start | bytes 18874372
  446.9 28.0 %copy-start.7 = (bf16[1,2,512,1024]{2,3,1,0:T(8,128)(2,1)}, bf16[1,2,512,1024]{2,3,1,0:T(8,128)(2,1)S(1)}, u32[]{:S(2)}) copy-start(bf16[1,2,512,1024]{2,3,1,0:T(8,128)(2,1)S(1)} %get-tuple-element.43) | copy-start | bytes 6291460
  496.7 50.0 %copy-start.10 = (f32[2,512,1024]{2,1,0:T(8,128)}, f32[2,512,1024]{2,1,0:T(8,128)S(1)}, u32[]{:S(2)}) copy-start(f32[2,512,1024]{2,1,0:T(8,128)S(1)} %get-tuple-element.74) | copy-start | bytes 12582916
  586.1 40.3 %copy-start.8 = (f32[2,512,1024]{2,1,0:T(8,128)}, f32[2,512,1024]{2,1,0:T(8,128)S(1)}, u32[]{:S(2)}) copy-start(f32[2,512,1024]{2,1,0:T(8,128)S(1)} %subtract_multiply_fusion) | copy-start | bytes 12582916
  586.1 24.3 copy-start.11
  636.4 25.8 %copy-start.5 = (bf16[2,512,1024]{1,2,0:T(8,128)(2,1)}, bf16[2,512,1024]{1,2,0:T(8,128)(2,1)S(1)}, u32[]{:S(2)}) copy-start(bf16[2,512,1024]{1,2,0:T(8,128)(2,1)S(1)} %copy.73) | copy-start | bytes 6291460
  662.2 28.4 %copy-start.1 = (bf16[1,2,512,1024]{2,3,1,0:T(8,128)(2,1)S(1)}, bf16[1,2,512,1024]{2,3,1,0:T(8,128)(2,1)}, u32[]{:S(2)}) copy-start(bf16[1,2,512,1024]{2,3,1,0:T(8,128)(2,1)} %copy-done) | copy-start | bytes 6291460
  729.7 23.3 copy-start.15
  729.7 23.3 copy-start.23
  729.7 23.3 copy-start.37
  729.7 23.3 copy-start.44
  729.7 23.3 copy-start.46
  729.7 23.3 copy-start.59
  729.7 23.3 copy-start.80
  794.1 1591.5 %reduce-scatter.2.cloned.1.call-start = ((), (), s32[]{:S(2)}) async-start(), calls=%async_computation.3 | async-start | bytes 69206016 | tf_op jit(solution)/shard_map/reduce_scatter | solution.py:301
  982.9 1406.1 %copy-start.99 = (f32[8]{0:T(128)S(1)}, f32[8]{0:T(128)}, u32[]{:S(2)}) copy-start(f32[8]{0:T(128)} %get-tuple-element.22) | copy-start | bytes 100
  982.9 1446.2 %copy-start.108 = (f32[8]{0:T(128)S(1)}, f32[8]{0:T(128)}, u32[]{:S(2)}) copy-start(f32[8]{0:T(128)} %copy-done.107) | copy-start | bytes 100
  982.9 1446.8 %copy-start.32 = (f32[2,6144]{1,0:T(2,128)S(1)}, f32[2,6144]{1,0:T(2,128)}, u32[]{:S(2)}) copy-start(f32[2,6144]{1,0:T(2,128)} %param.16) | copy-start | bytes 147460
  982.9 1446.8 %copy-start.34 = (f32[2,6144]{1,0:T(2,128)S(1)}, f32[2,6144]{1,0:T(2,128)}, u32[]{:S(2)}) copy-start(f32[2,6144]{1,0:T(2,128)} %param.18) | copy-start | bytes 147460
  982.9 1446.8 %copy-start.35 = (f32[2,6144]{1,0:T(2,128)S(1)}, f32[2,6144]{1,0:T(2,128)}, u32[]{:S(2)}) copy-start(f32[2,6144]{1,0:T(2,128)} %param.17) | copy-start | bytes 147460
  982.9 1448.6 %copy-start.19 = (f32[8,64,1024]{2,1,0:T(8,128)S(1)}, f32[8,64,1024]{2,1,0:T(8,128)}, u32[]{:S(2)}) copy-start(f32[8,64,1024]{2,1,0:T(8,128)} %param.13) | copy-start | bytes 6291460
  (71 other events, 619.6 us)
Sparse Core Ops, SparseCore 0:
  10.8 127.5 all-gather.3
  140.0 201.4 all-gather.5
  794.2 123.0 all-reduce.3
  983.0 1402.4 reduce-scatter.1
where the time goes:
time: 2450 us
  waiting for transfers between devices  1680 us (69%)
  matrix products  327 us (13%)
  local copies, waits for them, and re-layouts  239 us (10%)
  other arithmetic  94.4 us (4%)
  blocking collectives  85.5 us (3%)
    reduce_scatter x1, waiting for transfers between devices, per_device(): lax.psum_scatter(arranged, ('section', 'batch'), scatter_dimension=0, til...  1400 us
    all_gather x1, waiting for transfers between devices, per_device(): all_slots = lax.all_gather(shard_rows, 'section', axis=0, tiled=True)  152 us
    all_gather x1, waiting for transfers between devices, per_device(): lax.all_gather(masters.astype(jnp.bfloat16), 'batch', axis=1, tiled=True)  128 us
    scatter x1, local copies, waits for them, and re-layouts, per_device(): arranged.at[target_slot.reshape(-1)]  107 us
    dot_general x1, matrix products, forward(): jnp.einsum('rld,gde->rlge', input_two, up_w, preferred_element_type=float...  49.3 us
  transfers between devices with their start and end apart: 4, of which 3 were waited for; matrix products, arithmetic and copies ran while one was open for 8% of the time, Pallas kernels for 0%

commit v1 on v0

--- a/solution.py
+++ b/solution.py
@@ -1,3 +1,4 @@
+import functools
 import math
 import jax
 import jax.numpy as jnp
@@ -23,6 +24,40 @@
 pos_scale = 0.1
 exact = lax.Precision.HIGHEST
 float_out = jnp.float32
+
+
+def _direct_edge(unit, dim_no):
+    unit = jnp.moveaxis(unit, 0, dim_no)
+    base_arr = unit.shape
+    return unit.reshape(
+        *base_arr[:dim_no], base_arr[dim_no] * base_arr[dim_no + 1], *base_arr[dim_no + 2 :]
+    )
+
+
+def match_lane(local_x, lane_axis):
+    x_now = jax.lax.axis_size(lane_axis)
+    arr_next = jax.lax.axis_index(lane_axis)
+    wide_out, near = (x_now, arr_next)
+    o_now, r_now = (local_x[None], 1)
+    while r_now < wide_out:
+        small = range(wide_out)
+        u1 = map(lambda jj: (jj, jj ^ r_now), small)
+        res = list(u1)
+        main = jax.lax.ppermute(o_now, axis_name=lane_axis, perm=res)
+        w2 = near & r_now == 0
+        after = jnp.where(w2, o_now, main)
+        all_rows = jnp.where(w2, main, o_now)
+        o_now = jnp.concatenate([after, all_rows])
+        r_now *= 2
+    return o_now
+
+
+def pack_the_classes(matrix, packet, along_dim):
+    a_next = match_lane(matrix, packet)
+    return _direct_edge(a_next, along_dim)
+
+
+meet_the_words = functools.partial(pack_the_classes, packet="batch", along_dim=1)
 
 
 def positions(segs):
@@ -264,7 +299,7 @@
     row_count = section_ids.shape[0]
     section_hot = (section_ids[:, None] == jnp.arange(SECTIONS)[None, :]).astype(jnp.float32)
     local_counts = jnp.sum(section_hot, axis=0) * segments.shape[1]
-    shard_rows = lax.all_gather(masters.astype(jnp.bfloat16), "batch", axis=1, tiled=True)
+    shard_rows = meet_the_words(masters.astype(jnp.bfloat16))
     all_slots = lax.all_gather(shard_rows, "section", axis=0, tiled=True)
     blocks = jnp.take(all_slots, owners, axis=0)
     table = lax.all_gather(section_table, "section", axis=0, tiled=True)

time: 2450 us -> 2600 us (1.061)
  waiting for transfers between devices: 1680 us -> 1800 us
    ppermute x0 -> x3, waiting for transfers between devices: none -> 248 us  [match_lane(): main = jax.lax.ppermute(o_now, axis_name=lane_axis, perm=res)]
    all_gather x1 -> x0, waiting for transfers between devices: 128 us -> none  [per_device(): lax.all_gather(masters.astype(jnp.bfloat16), 'batch', axis=1, tiled=True)]
  transfers between devices with their start and end apart: 4 -> 6, of which waited for: 3 -> 5; matrix products, arithmetic and copies ran while one was open for 8% -> 7% of each run, Pallas kernels for 0% -> 0%
where the time goes in v1:
time: 2600 us; the launch traced here: 2590 us
  waiting for transfers between devices  1800 us (69%)
  matrix products  327 us (13%)
  local copies, waits for them, and re-layouts  240 us (9%)
  other arithmetic  113 us (4%)
  blocking collectives  86.5 us (3%)
    reduce_scatter x1, waiting for transfers between devices, per_device(): lax.psum_scatter(arranged, ('section', 'batch'), scatter_dimension=0, til...  1400 us
    ppermute x3, waiting for transfers between devices, match_lane(): main = jax.lax.ppermute(o_now, axis_name=lane_axis, perm=res)  248 us
    all_gather x1, waiting for transfers between devices, per_device(): all_slots = lax.all_gather(shard_rows, 'section', axis=0, tiled=True)  152 us
    scatter x1, local copies, waits for them, and re-layouts, per_device(): arranged.at[target_slot.reshape(-1)]  107 us
  transfers between devices with their start and end apart: 6, of which 5 were waited for; matrix products, arithmetic and copies ran while one was open for 7% of the time, Pallas kernels for 0%

profile of v1, /device:TPU:0, one launch (start us, length us, event | category | flops | bytes accessed | tf_op | source)
XLA Modules:
  0.0 2593.5 jit_solution(3504954028603516643)
XLA Ops:
  12.1 23.3 collective-permute-done
  39.9 45.1 %collective-permute-done.1 = bf16[2,8,64,1024]{3,2,0,1:T(8,128)(2,1)} collective-permute-done((bf16[2,8,64,1024]{3,2,0,1:T(8,128)(2,1)S(1)}, bf16[2,8,64,1024]{3,2,0,1:T(8,128)(2,1)}, u32[]{:S(2)}, u32[]{:S(2)}) %collective-permute-start.1) | collective-permute-done | bytes 2097184 | tf_op jit(solution)/shard_map/ppermute | solution.py:46
  92.3 179.4 %collective-permute-done.2 = bf16[4,8,64,1024]{3,2,0,1:T(8,128)(2,1)} collective-permute-done((bf16[4,8,64,1024]{3,2,0,1:T(8,128)(2,1)}, bf16[4,8,64,1024]{3,2,0,1:T(8,128)(2,1)}, u32[]{:S(2)}, u32[]{:S(2)}) %collective-permute-start.2) | collective-permute-done | bytes 4194336 | tf_op jit(solution)/shard_map/ppermute | solution.py:46
  271.7 5.4 broadcast_select_fusion.2
  277.2 7.4 pad_maximum_fusion
  285.4 39.7 %psum.28 = f32[8]{0:T(128)S(1)} all-reduce(f32[8]{0:T(128)S(1)} %broadcast_multiply_fusion.10), channel_id=1, replica_groups=mesh['section'=4,'batch'=8] {'section','batch'}, use_global_device_ids=true, to_apply=%region_13.14 | all-reduce | flops 8 | bytes 64 | tf_op jit(solution)/shard_map/psum | solution.py:313
  326.3 7.4 all-gather
  337.0 151.8 %all-gather.3.cloned.1.call-done = bf16[32,512,1024]{2,1,0:T(8,128)(2,1)} async-done(((bf16[8,512,1024]{2,1,0:T(8,128)(2,1)}), bf16[32,512,1024]{2,1,0:T(8,128)(2,1)}) %all-gather.3.cloned.1.call-update) | async-done | bytes 33554448 | tf_op jit(solution)/shard_map/all_gather | solution.py:303
  488.8 22.0 gather_fusion
  510.9 20.5 broadcast_select_fusion
  531.4 5.7 fusion.89
  540.6 14.0 fusion.88
  554.8 6.3 fusion.82
  561.1 17.8 fusion.92
  580.7 10.1 convert_bitcast_fusion
  594.1 13.7 fusion
  607.9 14.1 exponential_reduce_fusion
  622.1 15.6 convolution_convert_fusion.2
  637.7 6.3 fusion.93
  644.6 49.3 %multiply_convert_fusion.1 = (bf16[2,512,4,1024]{3,1,2,0:T(8,128)(2,1)}, f32[2,512,4,1024]{3,1,2,0:T(8,128)}, f32[2,512,4,1024]{3,1,2,0:T(8,128)}) fusion(bf16[4,1024,1024,1]{2,1,0,3:T(8,128)(2,1)S(1)} %bitcast.266, f32[2,512,1024]{2,1,0:T(8,128)S(1)} %get-tuple-element.80, f32[2,1024]{1,0:T(2,128)S(1)} %get-tuple-element.101, ...), kind=kOutput, calls=%fused_computation.14 | convolution fusion | flops 8867807232 | bytes 54550528 | tf_op jit(solution)/shard_map/rld,gde->rlge/dot_general | solution.py:151
  693.9 11.4 copy.71
  705.3 14.7 fusion.94
  728.1 4.0 multiply_reduce_fusion.1
  733.3 24.3 add_convert_fusion
  757.6 16.0 fusion.12
  777.1 3.7 convolution_convert_fusion.1
  783.7 25.7 multiply_reduce_fusion
  809.4 28.4 %multiply_convert_fusion = bf16[2,16,512,512]{2,3,1,0:T(8,128)(2,1)} fusion(f32[2,16,512,512]{2,3,1,0:T(8,128)} %get-tuple-element.89, f32[2,16,512,512]{2,3,1,0:T(8,128)} %get-tuple-element.78, f32[2,16,512]{2,1,0:T(8,128)S(1)} %get-tuple-element.88, f32[2,16,512]{2,1,0:T(8,128)S(1)} %copy-done.33, pred[2,512,512]{1,2,0:T(8,128)(4,1)S(1)} %copy-done.3), kind=kLoop, calls=%fused_computation.2 | loop fusion | flops 50331648 | bytes 84541440 | tf_op jit(solution)/shard_map/convert_element_type | solution.py:244
  837.8 9.9 multiply_convert_fusion.3
  847.7 13.0 multiply_convert_fusion.2
  860.7 16.2 convolution_convert_fusion
  877.0 23.3 fusion.76
  900.3 5.4 fusion.49
  908.2 4.1 copy.78
  912.3 3.9 copy.79
  916.2 14.8 fusion.23
  931.1 9.2 fusion.11
  941.6 5.5 add_convert_fusion.1
  947.3 5.5 fusion.80
  960.1 12.1 constant_dynamic-update-slice_fusion.1
  972.2 4.3 bitcast_dynamic-update-slice_fusion.1
  976.5 13.1 constant_dynamic-update-slice_fusion
  989.6 12.3 bitcast_dynamic-update-slice_fusion
  1001.9 21.3 broadcast_in_dim.46
  1023.2 106.9 %scatter_fusion = f32[256,64,1024]{2,1,0:T(8,128)} fusion(f32[256,64,1024]{2,1,0:T(8,128)} %broadcast_in_dim.46, s32[232]{0:T(256)S(1)} %bitcast.288, f32[232,64,1024]{2,1,0:T(8,128)} %bitcast.245), kind=kCustom, calls=%fused_computation.1 | custom fusion | bytes 182453152 | tf_op jit(solution)/shard_map/scatter | solution.py:335
  1133.3 1399.5 %reduce-scatter.2.cloned.1.call-done = f32[8,64,1024]{2,1,0:T(8,128)} async-done(((f32[256,64,1024]{2,1,0:T(8,128)}), f32[8,64,1024]{2,1,0:T(8,128)}) %reduce-scatter.2.cloned.1.call-update) | async-done | bytes 2097168 | tf_op jit(solution)/shard_map/reduce_scatter | solution.py:336
  2536.2 39.4 %all-reduce.1 = (f32[]{:T(128)}, f32[8]{0:T(128)S(1)}) all-reduce(f32[]{:T(128)S(6)} %add.310, f32[8]{0:T(128)S(1)} %copy-done.102), channel_id=1, replica_groups=mesh['section'=4,'batch'=8] {'section','batch'}, use_global_device_ids=true, to_apply=%region_33.34 | all-reduce | flops 9 | bytes 72 | tf_op jit(solution)/shard_map/psum | solution.py:338
  2578.7 6.9 multiply_subtract_fusion
  (331 shorter events, 64.1 us)
Async XLA Ops:
  7.2 28.2 %copy-start.5 = (f32[8,64,1024]{2,1,0:T(8,128)S(1)}, f32[8,64,1024]{2,1,0:T(8,128)}, u32[]{:S(2)}) copy-start(f32[8,64,1024]{2,1,0:T(8,128)} %param.13) | copy-start | bytes 6291460
  7.2 481.7 %all-gather.3.cloned.1.call-start = ((), (), s32[]{:S(2)}) async-start(), calls=%async_computation.1 | async-start | bytes 41943040 | tf_op jit(solution)/shard_map/all_gather | solution.py:303
  9.1 26.3 %collective-permute-start = (bf16[1,8,64,1024]{3,2,0,1:T(8,128)(2,1)S(1)}, bf16[1,8,64,1024]{3,2,0,1:T(8,128)(2,1)}, u32[]{:S(2)}, u32[]{:S(2)}) collective-permute-start(bf16[1,8,64,1024]{3,2,0,1:T(8,128)(2,1)S(1)} %convert_bitcast_fusion.1), channel_id=1, source_target_pairs={{0,1},{1,0},{2,3},{3,2},{4,5},{5,4},{6,7},{7,6},{8,9},{9,8},{10,11... | collective-permute-start | bytes 3145736 | tf_op jit(solution)/shard_map/ppermute | solution.py:46
  38.0 47.0 %collective-permute-start.1 = (bf16[2,8,64,1024]{3,2,0,1:T(8,128)(2,1)S(1)}, bf16[2,8,64,1024]{3,2,0,1:T(8,128)(2,1)}, u32[]{:S(2)}, u32[]{:S(2)}) collective-permute-start(bf16[2,8,64,1024]{3,2,0,1:T(8,128)(2,1)S(1)} %pad_maximum_fusion.5), channel_id=1, source_target_pairs={{0,2},{1,3},{2,0},{3,1},{4,6},{5,7},{6,4},{7,5},{8,10},{9,11},{10,... | collective-permute-start | bytes 6291464 | tf_op jit(solution)/shard_map/ppermute | solution.py:46
  89.8 181.9 %collective-permute-start.2 = (bf16[4,8,64,1024]{3,2,0,1:T(8,128)(2,1)}, bf16[4,8,64,1024]{3,2,0,1:T(8,128)(2,1)}, u32[]{:S(2)}, u32[]{:S(2)}) collective-permute-start(bf16[4,8,64,1024]{3,2,0,1:T(8,128)(2,1)} %pad_maximum_fusion.2), channel_id=1, source_target_pairs={{0,4},{1,5},{2,6},{3,7},{4,0},{5,1},{6,2},{7,3},{8,12},{9,13},{10,... | collective-permute-start | bytes 12582920 | tf_op jit(solution)/shard_map/ppermute | solution.py:46
  284.6 40.5 %copy-start.36 = (s32[2,512]{1,0:T(2,128)S(1)}, s32[2,512]{1,0:T(2,128)}, u32[]{:S(2)}) copy-start(s32[2,512]{1,0:T(2,128)} %param.23) | copy-start | bytes 12292
  284.6 41.7 %copy-start.34 = (f32[2,6144]{1,0:T(2,128)S(1)}, f32[2,6144]{1,0:T(2,128)}, u32[]{:S(2)}) copy-start(f32[2,6144]{1,0:T(2,128)} %param.16) | copy-start | bytes 147460
  284.6 49.6 %copy-start.106 = (s32[29]{0:T(128)S(1)}, s32[29]{0:T(128)}, u32[]{:S(2)}) copy-start(s32[29]{0:T(128)} %param.19) | copy-start | bytes 352
  284.6 51.1 %copy-start.45 = (s32[2,512,8]{1,2,0:T(8,128)S(1)}, s32[2,512,8]{1,2,0:T(8,128)}, u32[]{:S(2)}) copy-start(s32[2,512,8]{1,2,0:T(8,128)} %param.22) | copy-start | bytes 98308
  284.6 846.4 %all-reduce.4.cloned.1.call-start = ((), (), s32[]{:S(2)}) async-start(), calls=%async_computation.3 | async-start | bytes 393216 | tf_op jit(solution)/shard_map/psum | solution.py:319
  335.6 219.1 %copy-start.86 = (bf16[2]{0:T(256)(128)(2,1)}, bf16[2]{0:T(256)(128)(2,1)S(1)}, u32[]{:S(2)}) copy-start(bf16[2]{0:T(256)(128)(2,1)S(1)} %get-tuple-element.64) | copy-start | bytes 16
  335.6 219.1 %copy-start.88 = (bf16[2]{0:T(256)(128)(2,1)}, bf16[2]{0:T(256)(128)(2,1)S(1)}, u32[]{:S(2)}) copy-start(bf16[2]{0:T(256)(128)(2,1)S(1)} %get-tuple-element.65) | copy-start | bytes 16
  335.6 219.1 %copy-start.90 = (bf16[2]{0:T(256)(128)(2,1)}, bf16[2]{0:T(256)(128)(2,1)S(1)}, u32[]{:S(2)}) copy-start(bf16[2]{0:T(256)(128)(2,1)S(1)} %get-tuple-element.66) | copy-start | bytes 16
  335.6 219.1 %copy-start.92 = (bf16[2]{0:T(256)(128)(2,1)}, bf16[2]{0:T(256)(128)(2,1)S(1)}, u32[]{:S(2)}) copy-start(bf16[2]{0:T(256)(128)(2,1)S(1)} %get-tuple-element.67) | copy-start | bytes 16
  335.6 219.1 %copy-start.94 = (bf16[2]{0:T(256)(128)(2,1)}, bf16[2]{0:T(256)(128)(2,1)S(1)}, u32[]{:S(2)}) copy-start(bf16[2]{0:T(256)(128)(2,1)S(1)} %get-tuple-element.68) | copy-start | bytes 16
  335.6 219.1 %copy-start.96 = (bf16[2]{0:T(256)(128)(2,1)}, bf16[2]{0:T(256)(128)(2,1)S(1)}, u32[]{:S(2)}) copy-start(bf16[2]{0:T(256)(128)(2,1)S(1)} %get-tuple-element.69) | copy-start | bytes 16
  335.6 219.1 %copy-start.98 = (bf16[2]{0:T(256)(128)(2,1)}, bf16[2]{0:T(256)(128)(2,1)S(1)}, u32[]{:S(2)}) copy-start(bf16[2]{0:T(256)(128)(2,1)S(1)} %get-tuple-element.70) | copy-start | bytes 16
  335.6 219.1 %copy-start.100 = (bf16[2]{0:T(256)(128)(2,1)}, bf16[2]{0:T(256)(128)(2,1)S(1)}, u32[]{:S(2)}) copy-start(bf16[2]{0:T(256)(128)(2,1)S(1)} %get-tuple-element.71) | copy-start | bytes 16
  335.8 218.9 %copy-start.66 = (s32[2,512]{1,0:T(2,128)}, s32[2,512]{1,0:T(2,128)S(1)}, u32[]{:S(2)}) copy-start(s32[2,512]{1,0:T(2,128)S(1)} %get-tuple-element.91) | copy-start | bytes 12292
  335.8 218.9 %copy-start.68 = (s32[2,512]{1,0:T(2,128)}, s32[2,512]{1,0:T(2,128)S(1)}, u32[]{:S(2)}) copy-start(s32[2,512]{1,0:T(2,128)S(1)} %get-tuple-element.92) | copy-start | bytes 12292
  335.8 218.9 %copy-start.70 = (s32[2,512]{1,0:T(2,128)}, s32[2,512]{1,0:T(2,128)S(1)}, u32[]{:S(2)}) copy-start(s32[2,512]{1,0:T(2,128)S(1)} %get-tuple-element.93) | copy-start | bytes 12292
  335.8 218.9 %copy-start.72 = (s32[2,512]{1,0:T(2,128)}, s32[2,512]{1,0:T(2,128)S(1)}, u32[]{:S(2)}) copy-start(s32[2,512]{1,0:T(2,128)S(1)} %get-tuple-element.94) | copy-start | bytes 12292
  335.9 218.9 %copy-start.74 = (s32[2,512]{1,0:T(2,128)}, s32[2,512]{1,0:T(2,128)S(1)}, u32[]{:S(2)}) copy-start(s32[2,512]{1,0:T(2,128)S(1)} %get-tuple-element.95) | copy-start | bytes 12292
  335.9 218.9 %copy-start.76 = (s32[2,512]{1,0:T(2,128)}, s32[2,512]{1,0:T(2,128)S(1)}, u32[]{:S(2)}) copy-start(s32[2,512]{1,0:T(2,128)S(1)} %get-tuple-element.96) | copy-start | bytes 12292
  335.9 218.9 %copy-start.78 = (s32[2,512]{1,0:T(2,128)}, s32[2,512]{1,0:T(2,128)S(1)}, u32[]{:S(2)}) copy-start(s32[2,512]{1,0:T(2,128)S(1)} %get-tuple-element.97) | copy-start | bytes 12292
  335.9 218.9 %copy-start.80 = (s32[2,512]{1,0:T(2,128)}, s32[2,512]{1,0:T(2,128)S(1)}, u32[]{:S(2)}) copy-start(s32[2,512]{1,0:T(2,128)S(1)} %get-tuple-element.98) | copy-start | bytes 12292
  336.0 243.5 %copy-start.43 = (f32[2,1024]{1,0:T(2,128)}, f32[2,1024]{1,0:T(2,128)S(1)}, u32[]{:S(2)}) copy-start(f32[2,1024]{1,0:T(2,128)S(1)} %get-tuple-element.104) | copy-start | bytes 24580
  336.0 243.5 %copy-start.59 = (f32[2,1024]{1,0:T(2,128)}, f32[2,1024]{1,0:T(2,128)S(1)}, u32[]{:S(2)}) copy-start(f32[2,1024]{1,0:T(2,128)S(1)} %get-tuple-element.103) | copy-start | bytes 24580
  336.0 308.5 %copy-start.63 = (f32[2,1024]{1,0:T(2,128)}, f32[2,1024]{1,0:T(2,128)S(1)}, u32[]{:S(2)}) copy-start(f32[2,1024]{1,0:T(2,128)S(1)} %get-tuple-element.101) | copy-start | bytes 24580
  337.0 285.1 %copy-start.2 = (pred[2,512,512]{1,2,0:T(8,128)(4,1)}, pred[2,512,512]{1,2,0:T(8,128)(4,1)S(1)}, u32[]{:S(2)}) copy-start(pred[2,512,512]{1,2,0:T(8,128)(4,1)S(1)} %broadcast_compare_fusion) | copy-start | bytes 1572868
  540.6 38.9 %copy-start.23 = (bf16[6,512,1024]{2,1,0:T(8,128)(2,1)}, bf16[6,512,1024]{2,1,0:T(8,128)(2,1)S(1)}, u32[]{:S(2)}) copy-start(bf16[6,512,1024]{2,1,0:T(8,128)(2,1)S(1)} %slice.160) | copy-start | bytes 18874372
  594.1 28.0 %copy-start.10 = (bf16[1,2,512,1024]{2,3,1,0:T(8,128)(2,1)}, bf16[1,2,512,1024]{2,3,1,0:T(8,128)(2,1)S(1)}, u32[]{:S(2)}) copy-start(bf16[1,2,512,1024]{2,3,1,0:T(8,128)(2,1)S(1)} %get-tuple-element.45) | copy-start | bytes 6291460
  644.0 49.9 %copy-start.13 = (f32[2,512,1024]{2,1,0:T(8,128)}, f32[2,512,1024]{2,1,0:T(8,128)S(1)}, u32[]{:S(2)}) copy-start(f32[2,512,1024]{2,1,0:T(8,128)S(1)} %get-tuple-element.80) | copy-start | bytes 12582916
  733.3 40.3 %copy-start.11 = (f32[2,512,1024]{2,1,0:T(8,128)}, f32[2,512,1024]{2,1,0:T(8,128)S(1)}, u32[]{:S(2)}) copy-start(f32[2,512,1024]{2,1,0:T(8,128)S(1)} %subtract_multiply_fusion) | copy-start | bytes 12582916
  733.3 24.3 copy-start.14
  783.7 25.7 copy-start.8
  809.4 28.4 %copy-start.1 = (bf16[1,2,512,1024]{2,3,1,0:T(8,128)(2,1)S(1)}, bf16[1,2,512,1024]{2,3,1,0:T(8,128)(2,1)}, u32[]{:S(2)}) copy-start(bf16[1,2,512,1024]{2,3,1,0:T(8,128)(2,1)} %copy-done) | copy-start | bytes 6291460
  876.9 23.4 copy-start.18
  876.9 23.4 copy-start.26
  876.9 23.4 copy-start.40
  876.9 23.4 copy-start.47
  941.4 1591.4 %reduce-scatter.2.cloned.1.call-start = ((), (), s32[]{:S(2)}) async-start(), calls=%async_computation.2 | async-start | bytes 69206016 | tf_op jit(solution)/shard_map/reduce_scatter | solution.py:336
  1130.1 1406.1 %copy-start.102 = (f32[8]{0:T(128)S(1)}, f32[8]{0:T(128)}, u32[]{:S(2)}) copy-start(f32[8]{0:T(128)} %get-tuple-element.22) | copy-start | bytes 100
  1130.1 1446.1 %copy-start.111 = (f32[8]{0:T(128)S(1)}, f32[8]{0:T(128)}, u32[]{:S(2)}) copy-start(f32[8]{0:T(128)} %copy-done.110) | copy-start | bytes 100
  1130.1 1446.8 %copy-start.35 = (f32[2,6144]{1,0:T(2,128)S(1)}, f32[2,6144]{1,0:T(2,128)}, u32[]{:S(2)}) copy-start(f32[2,6144]{1,0:T(2,128)} %param.16) | copy-start | bytes 147460
  1130.1 1446.8 %copy-start.37 = (f32[2,6144]{1,0:T(2,128)S(1)}, f32[2,6144]{1,0:T(2,128)}, u32[]{:S(2)}) copy-start(f32[2,6144]{1,0:T(2,128)} %param.18) | copy-start | bytes 147460
  1130.1 1446.8 %copy-start.38 = (f32[2,6144]{1,0:T(2,128)S(1)}, f32[2,6144]{1,0:T(2,128)}, u32[]{:S(2)}) copy-start(f32[2,6144]{1,0:T(2,128)} %param.17) | copy-start | bytes 147460
  1130.1 1448.6 %copy-start.6 = (f32[8,64,1024]{2,1,0:T(8,128)S(1)}, f32[8,64,1024]{2,1,0:T(8,128)}, u32[]{:S(2)}) copy-start(f32[8,64,1024]{2,1,0:T(8,128)} %param.13) | copy-start | bytes 6291460
  (76 other events, 693.0 us)
Sparse Core Ops, SparseCore 0:
  284.8 204.0 all-gather.2
  941.5 123.0 all-reduce.3
  1130.3 1402.4 reduce-scatter.1
